TPU v7x, 256 devices: a whole 4x4x8 slice. The times are simulated.
256 devices in a mesh: fsdp: 32 (over z_hi, x, core), dp: 8 (over y, z_lo).
Axes of the slice: x: 4, y: 4, z: 8 (z_hi: 4, z_lo: 2; z = z_hi * 2 + z_lo), core: 2. Of those that a mesh axis runs over, the one named last changes fastest.
Arguments:
- activations: bfloat16 [65536, 4096], P(('fsdp', 'dp')), may hold values from -6 to 6
- cotangents: bfloat16 [2, 65536, 4096], P(None, ('fsdp', 'dp')), may hold values from -6 to 6
- weights: bfloat16 [2, 4096, 4096], P(None, 'fsdp'), may hold values from -4 to 4
- projectors: bfloat16 [2, 4096, 512], P(None, 'fsdp'), may hold values from -0.09375 to 0.09375
- first_moment: float32 [2, 4096, 512], P(None, 'fsdp'), may hold values from -3 to 3
- second_moment: float32 [2, 4096, 512], P(None, 'fsdp'), may hold values from 0.25 to 4
- matrix_settings: int32 [2, 2], replicated, may hold values from 0 to 512, as said below
Outputs:
- new_weights: bfloat16 [2, 4096, 4096], P(None, 'fsdp')
- new_first: float32 [2, 4096, 512], P(None, 'fsdp')
- new_second: float32 [2, 4096, 512], P(None, 'fsdp')
Inputs may be any that keep to these rules, and one draw needn't show every extreme that they name: `matrix_settings`: column 0 is a rank from 128 to 512, some matrix has rank exactly 512; column 1 is 0 (the projector acts on the activations) or 1 (on the cotangents), and both values occur.
All inputs are finite; a program needn't handle non-finite values.
Results may differ from a plain program's by a relative error of at most 0.0045.
Values may be sent and summed in bfloat16 or wider, within the bound.
No kernel may reach another device: no remote copies, remote signals or barrier semaphores. Data moves between devices by JAX's collectives and lax.ppermute only.
A program may use at most 128 MiB of HBM per device.

v0:
```python
import math
import jax
import jax.numpy as jnp
from jax import lax
from jax.sharding import PartitionSpec as P

BETA_ONE = 0.9
BETA_TWO = 0.95
EPSILON = 1e-08


def on_device(
    activations, cotangents, weights, projectors, first_moment, second_moment, matrix_settings
):
    rank_max = projectors.shape[2]
    token_local = activations.shape[0]
    token_total = token_local * lax.axis_size("fsdp") * lax.axis_size("dp")
    grad_scale = 1.0 / math.sqrt(token_total)
    rank_columns = jnp.arange(rank_max)
    weight_list, first_list, second_list = ([], [], [])
    for matrix_index in range(cotangents.shape[0]):
        live_mask = (rank_columns < matrix_settings[matrix_index, 0])[None, :]
        on_inputs = matrix_settings[matrix_index, 1] == 0
        proj_local = jnp.where(live_mask, projectors[matrix_index], jnp.zeros((), jnp.bfloat16))
        grads_out = cotangents[matrix_index]
        projected_side = jnp.where(on_inputs, activations, grads_out)
        other_side = jnp.where(on_inputs, grads_out, activations)
        shard_piece = lax.all_gather(proj_local, "fsdp", axis=0, tiled=True)
        coeff_sum = jnp.dot(projected_side, shard_piece, preferred_element_type=jnp.float32)
        coeff_sum, full_projector = (coeff_sum, shard_piece)
        coeffs = coeff_sum.astype(jnp.bfloat16)
        partial_sums = lax.psum_scatter(
            lax.dot_general(
                other_side, coeffs, (((0,), (0,)), ((), ())), preferred_element_type=jnp.float32
            ),
            "fsdp",
            scatter_dimension=0,
            tiled=True,
        )
        projected = (
            lax.psum(partial_sums.astype(jnp.bfloat16), "dp").astype(jnp.float32) * grad_scale
        )
        moment_one = jnp.where(
            live_mask, BETA_ONE * first_moment[matrix_index] + (1.0 - BETA_ONE) * projected, 0.0
        )
        moment_two = jnp.where(
            live_mask,
            BETA_TWO * second_moment[matrix_index] + (1.0 - BETA_TWO) * projected * projected,
            0.0,
        )
        normalized = jnp.where(
            live_mask, moment_one / (jnp.sqrt(moment_two) + EPSILON), 0.0
        ).astype(jnp.bfloat16)
        update = lax.dot_general(
            normalized, full_projector, (((1,), (1,)), ((), ())), preferred_element_type=jnp.float32
        )
        weight_list.append(
            (weights[matrix_index].astype(jnp.float32) - update).astype(jnp.bfloat16)
        )
        first_list.append(moment_one)
        second_list.append(moment_two)
    return (jnp.stack(weight_list), jnp.stack(first_list), jnp.stack(second_list))


def solution(mesh):
    return jax.shard_map(
        on_device,
        mesh=mesh,
        in_specs=(
            P(("fsdp", "dp"), None),
            P(None, ("fsdp", "dp"), None),
            P(None, "fsdp", None),
            P(None, "fsdp", None),
            P(None, "fsdp", None),
            P(None, "fsdp", None),
            P(),
        ),
        out_specs=(P(None, "fsdp", None), P(None, "fsdp", None), P(None, "fsdp", None)),
        check_vma=False,
    )
```

profile of v0, /device:TPU:2, one launch (start us, length us, event | category | flops | bytes accessed | tf_op | source)
XLA Modules:
  0.0 480.4 jit_solution(6036514137004158276)
XLA Ops:
  7.2 1.5 fusion.56
  8.7 1.3 iota_compare_fusion
  10.0 1.7 bitcast_select_fusion.17
  11.7 0.0 all-gather.3.cloned.1.call-start
  11.8 0.7 all-gather.3.cloned.1.call-update
  12.5 0.0 reduce-scatter.5.cloned.1.call-start
  13.2 61.6 %all-gather.5.cloned.1.call-done = bf16[4096,512]{1,0:T(8,128)(2,1)} async-done(((bf16[128,512]{1,0:T(8,128)(2,1)}), bf16[4096,512]{1,0:T(8,128)(2,1)}) %all-gather.5.cloned.1.call-update) | async-done | bytes 4194320 | tf_op jit(solution)/shard_map/all_gather | solution.py:28
  74.8 9.8 %fusion.4 = f32[4096,512]{1,0:T(8,128)} fusion(bf16[256,4096]{1,0:T(8,128)(2,1)} %param.7, pred[]{:T(512)} %bitcast.11, bf16[2,256,4096]{2,1,0:T(8,128)(2,1)} %param.8, bf16[4096,512]{1,0:T(8,128)(2,1)} %all-gather.5.cloned.1.call-done), kind=kOutput, calls=%fused_computation.9 | convolution fusion | flops 2149711872 | bytes 20972544 | tf_op jit(solution)/shard_map/dot_general | solution.py:33
  84.6 0.0 reduce-scatter.3.cloned.1.call-start
  85.5 50.9 %all-gather.3.cloned.1.call-done = bf16[4096,512]{1,0:T(8,128)(2,1)} async-done(((bf16[128,512]{1,0:T(8,128)(2,1)}), bf16[4096,512]{1,0:T(8,128)(2,1)}) %all-gather.3.cloned.1.call-update) | async-done | bytes 4194320 | tf_op jit(solution)/shard_map/all_gather | solution.py:28
  136.4 9.2 %fusion.6 = f32[4096,512]{1,0:T(8,128)} fusion(bf16[256,4096]{1,0:T(8,128)(2,1)S(1)} %copy-done, pred[]{:T(512)} %bitcast.3, bf16[2,256,4096]{2,1,0:T(8,128)(2,1)} %param.8, bf16[4096,512]{1,0:T(8,128)(2,1)} %all-gather.3.cloned.1.call-done), kind=kOutput, calls=%fused_computation.13 | convolution fusion | flops 2149711872 | bytes 20972544 | tf_op jit(solution)/shard_map/dot_general | solution.py:33
  145.6 0.0 all-reduce.3.cloned.1.call-start
  145.7 113.7 %reduce-scatter.5.cloned.1.call-done = f32[128,512]{1,0:T(8,128)} async-done(((f32[4096,512]{1,0:T(8,128)}), f32[128,512]{1,0:T(8,128)}) %reduce-scatter.5.cloned.1.call-update) | async-done | bytes 262160 | tf_op jit(solution)/shard_map/reduce_scatter | solution.py:32
  259.4 1.6 convert_element_type.52
  261.0 121.5 %reduce-scatter.3.cloned.1.call-done = f32[128,512]{1,0:T(8,128)} async-done(((f32[4096,512]{1,0:T(8,128)}), f32[128,512]{1,0:T(8,128)}) %reduce-scatter.3.cloned.1.call-update) | async-done | bytes 262160 | tf_op jit(solution)/shard_map/reduce_scatter | solution.py:32
  382.5 1.6 convert_element_type.45
  384.2 79.3 %all-reduce.3.cloned.1.call-done = (bf16[128,512]{1,0:T(8,128)(2,1)}, bf16[128,512]{1,0:T(8,128)(2,1)}) async-done(((bf16[128,512]{1,0:T(8,128)(2,1)}, bf16[128,512]{1,0:T(8,128)(2,1)}), (bf16[128,512]{1,0:T(8,128)(2,1)}, bf16[128,512]{1,0:T(8,128)(2,1)})) %all-reduce.3.cloned.1.call-update) | async-done | bytes 262160 | tf_op jit(solution)/shard_map/psum | solution.py:41
  463.5 1.2 fusion.36
  464.8 4.1 fusion.3
  468.9 0.3 copy-done.6
  469.2 1.5 fusion.2
  470.7 1.5 pad_maximum_fusion
  472.2 0.8 pad_maximum_fusion.1
  473.0 0.8 pad_maximum_fusion.2
  (18 shorter events, 0.1 us)
Async XLA Ops:
  7.2 67.7 %all-gather.5.cloned.1.call-start = ((), (), s32[]{:S(2)}) async-start(), calls=%async_computation.4 | async-start | bytes 4325376 | tf_op jit(solution)/shard_map/all_gather | solution.py:28
  11.7 124.7 %all-gather.3.cloned.1.call-start = ((), (), s32[]{:S(2)}) async-start(), calls=%async_computation.2 | async-start | bytes 4325376 | tf_op jit(solution)/shard_map/all_gather | solution.py:28
  12.5 246.9 %reduce-scatter.5.cloned.1.call-start = ((), (), s32[]{:S(2)}) async-start(), calls=%async_computation.5 | async-start | bytes 8650752 | tf_op jit(solution)/shard_map/reduce_scatter | solution.py:32
  84.6 51.8 %copy-start = (bf16[256,4096]{1,0:T(8,128)(2,1)S(1)}, bf16[256,4096]{1,0:T(8,128)(2,1)}, u32[]{:S(2)}) copy-start(bf16[256,4096]{1,0:T(8,128)(2,1)} %param.7) | copy-start | bytes 6291460
  84.6 297.9 %reduce-scatter.3.cloned.1.call-start = ((), (), s32[]{:S(2)}) async-start(), calls=%async_computation.3 | async-start | bytes 8650752 | tf_op jit(solution)/shard_map/reduce_scatter | solution.py:32
  145.6 317.9 %copy-start.2 = (f32[2,128,512]{2,1,0:T(8,128)S(1)}, f32[2,128,512]{2,1,0:T(8,128)}, u32[]{:S(2)}) copy-start(f32[2,128,512]{2,1,0:T(8,128)} %param.11) | copy-start | bytes 1572868
  145.6 317.9 %copy-start.3 = (f32[2,128,512]{2,1,0:T(8,128)S(1)}, f32[2,128,512]{2,1,0:T(8,128)}, u32[]{:S(2)}) copy-start(f32[2,128,512]{2,1,0:T(8,128)} %param.12) | copy-start | bytes 1572868
  145.6 317.9 %all-reduce.3.cloned.1.call-start = ((), (), s32[]{:S(2)}) async-start(), calls=%async_computation.6 | async-start | bytes 524288 | tf_op jit(solution)/shard_map/psum | solution.py:41
  463.5 1.2 copy-start.5
  464.7 4.2 copy-start.1
  464.7 4.2 copy-start.4
  464.8 4.5 copy-start.6
Sparse Core Ops, SparseCore 0:
  11.8 62.9 all-gather.4
  78.0 58.3 all-gather.2
  140.4 118.9 reduce-scatter.4
  263.3 119.2 reduce-scatter.2
  385.6 77.8 all-reduce.2
where the time goes:
time: 481 us; the launch traced here: 480 us
  waiting for transfers between devices  428 us (89%)
  matrix products  24.5 us (5%)
  between operations  15.3 us (3%)
  other arithmetic  10.6 us (2%)
    reduce_scatter x2, waiting for transfers between devices, on_device(): lax.psum_scatter(lax.dot_general(other_side, coeffs, (((0,), (0,)), ((),...  235 us
    all_gather x2, waiting for transfers between devices, on_device(): shard_piece = lax.all_gather(proj_local, 'fsdp', axis=0, tiled=True)  113 us
    psum x1, waiting for transfers between devices, on_device(): lax.psum(partial_sums.astype(jnp.bfloat16), 'dp').astype(jnp.float32)  79.3 us
    dot_general x2, matrix products, on_device(): lax.dot_general(other_side, coeffs, (((0,), (0,)), ((), ())), preferred_e...  18.9 us
  transfers between devices with their start and end apart: 5, of which 5 were waited for; matrix products, arithmetic and copies ran while one was open for 4% of the time, Pallas kernels for 0%

commit v1 on v0

--- a/solution.py
+++ b/solution.py
@@ -25,7 +25,10 @@
         grads_out = cotangents[matrix_index]
         projected_side = jnp.where(on_inputs, activations, grads_out)
         other_side = jnp.where(on_inputs, grads_out, activations)
-        shard_piece = lax.all_gather(proj_local, "fsdp", axis=0, tiled=True)
+        count = lax.axis_size("fsdp")
+        blocks = jnp.stack([proj_local for _ in range(count)])
+        blocks = lax.all_to_all(blocks, "fsdp", split_axis=0, concat_axis=0)
+        shard_piece = jnp.concatenate(blocks, axis=0)
         coeff_sum = jnp.dot(projected_side, shard_piece, preferred_element_type=jnp.float32)
         coeff_sum, full_projector = (coeff_sum, shard_piece)
         coeffs = coeff_sum.astype(jnp.bfloat16)

time: 481 us -> 517 us (1.075)
  starting transfers between devices: 0.2 us -> 17.4 us
  waiting for transfers between devices: 428 us -> 442 us
    all_to_all x0 -> x2, waiting for transfers between devices: none -> 223 us  [on_device(): blocks = lax.all_to_all(blocks, 'fsdp', split_axis=0, concat_axis=0)]
    all_gather x2 -> x0, waiting for transfers between devices: 113 us -> none  [on_device(): shard_piece = lax.all_gather(proj_local, 'fsdp', axis=0, tiled=True)]
    reduce_scatter x2, waiting for transfers between devices: 235 us -> 139 us  [on_device(): lax.psum_scatter(lax.dot_general(other_side, coeffs, (((0,), (0,)), ((),...]
    all_to_all x0 -> x2, starting transfers between devices: none -> 17.3 us  [on_device(): blocks = lax.all_to_all(blocks, 'fsdp', split_axis=0, concat_axis=0)]
  transfers between devices with their start and end apart: 5 -> 5, of which waited for: 5 -> 5; matrix products, arithmetic and copies ran while one was open for 4% -> 3% of each run, Pallas kernels for 0% -> 0%
where the time goes in v1:
time: 517 us; the launch traced here: 516 us
  waiting for transfers between devices  442 us (85%)
  matrix products  26.3 us (5%)
  starting transfers between devices  17.4 us (3%)
  between operations  15.1 us (3%)
  other arithmetic  8.88 us (2%)
  local copies, waits for them, and re-layouts  6.33 us (1%)
    all_to_all x2, waiting for transfers between devices, on_device(): blocks = lax.all_to_all(blocks, 'fsdp', split_axis=0, concat_axis=0)  223 us
    reduce_scatter x2, waiting for transfers between devices, on_device(): lax.psum_scatter(lax.dot_general(other_side, coeffs, (((0,), (0,)), ((),...  139 us
    psum x1, waiting for transfers between devices, on_device(): lax.psum(partial_sums.astype(jnp.bfloat16), 'dp').astype(jnp.float32)  79.6 us
    dot_general x2, matrix products, on_device(): lax.dot_general(other_side, coeffs, (((0,), (0,)), ((), ())), preferred_e...  18.4 us
    all_to_all x2, starting transfers between devices, on_device(): blocks = lax.all_to_all(blocks, 'fsdp', split_axis=0, concat_axis=0)  17.3 us
  transfers between devices with their start and end apart: 5, of which 5 were waited for; matrix products, arithmetic and copies ran while one was open for 3% of the time, Pallas kernels for 0%

profile of v1, /device:TPU:2, one launch (start us, length us, event | category | flops | bytes accessed | tf_op | source)
XLA Modules:
  0.0 516.2 jit_solution(11248932307391856240)
XLA Ops:
  7.2 1.4 fusion.56
  8.6 1.3 iota_compare_fusion
  9.9 1.0 select_bitcast_fusion.1
  10.9 2.4 stack.30
  13.3 11.8 %all-to-all-start.1 = ((bf16[32,128,512]{2,1,0:T(8,128)(2,1)}), bf16[32,128,512]{2,1,0:T(8,128)(2,1)}, u32[]{:S(2)}, u32[]{:S(2)}) async-start(bf16[32,128,512]{2,1,0:T(8,128)(2,1)} %stack.30), calls=%async_computation.2 | async-start | bytes 8388608 | tf_op jit(solution)/shard_map/all_to_all | solution.py:30
  25.8 95.3 %all-to-all-done.1 = bf16[32,128,512]{2,1,0:T(8,128)(2,1)} async-done(((bf16[32,128,512]{2,1,0:T(8,128)(2,1)}), bf16[32,128,512]{2,1,0:T(8,128)(2,1)}, u32[]{:S(2)}, u32[]{:S(2)}) %all-to-all-start.1) | async-done | bytes 4194336 | tf_op jit(solution)/shard_map/all_to_all | solution.py:30
  121.1 9.2 %fusion.4 = f32[4096,512]{1,0:T(8,128)} fusion(bf16[256,4096]{1,0:T(8,128)(2,1)S(1)} %copy-done, pred[]{:T(512)} %bitcast.12, bf16[2,256,4096]{2,1,0:T(8,128)(2,1)} %param.8, bf16[4096,512]{1,0:T(8,128)(2,1)} %bitcast.15), kind=kOutput, calls=%fused_computation.9 | convolution fusion | flops 2149711872 | bytes 20972544 | tf_op jit(solution)/shard_map/dot_general | solution.py:36
  130.3 2.4 stack.27
  132.7 5.5 %all-to-all-start = ((bf16[32,128,512]{2,1,0:T(8,128)(2,1)}), bf16[32,128,512]{2,1,0:T(8,128)(2,1)}, u32[]{:S(2)}, u32[]{:S(2)}) async-start(bf16[32,128,512]{2,1,0:T(8,128)(2,1)} %stack.27), calls=%async_computation | async-start | bytes 8388608 | tf_op jit(solution)/shard_map/all_to_all | solution.py:30
  138.2 0.0 reduce-scatter.3.cloned.1.call-start
  138.9 128.1 %all-to-all-done = bf16[32,128,512]{2,1,0:T(8,128)(2,1)} async-done(((bf16[32,128,512]{2,1,0:T(8,128)(2,1)}), bf16[32,128,512]{2,1,0:T(8,128)(2,1)}, u32[]{:S(2)}, u32[]{:S(2)}) %all-to-all-start) | async-done | bytes 4194336 | tf_op jit(solution)/shard_map/all_to_all | solution.py:30
  267.0 9.2 %fusion.6 = f32[4096,512]{1,0:T(8,128)} fusion(bf16[256,4096]{1,0:T(8,128)(2,1)S(1)} %copy-done, pred[]{:T(512)} %bitcast.3, bf16[2,256,4096]{2,1,0:T(8,128)(2,1)} %param.8, bf16[4096,512]{1,0:T(8,128)(2,1)} %bitcast.6), kind=kOutput, calls=%fused_computation.13 | convolution fusion | flops 2149711872 | bytes 20972544 | tf_op jit(solution)/shard_map/dot_general | solution.py:36
  276.3 0.0 all-reduce.3.cloned.1.call-start
  276.4 17.3 %reduce-scatter.5.cloned.1.call-done = f32[128,512]{1,0:T(8,128)} async-done(((f32[4096,512]{1,0:T(8,128)}), f32[128,512]{1,0:T(8,128)}) %reduce-scatter.5.cloned.1.call-update) | async-done | bytes 262160 | tf_op jit(solution)/shard_map/reduce_scatter | solution.py:35
  293.7 1.6 convert_element_type.52
  295.3 121.8 %reduce-scatter.3.cloned.1.call-done = f32[128,512]{1,0:T(8,128)} async-done(((f32[4096,512]{1,0:T(8,128)}), f32[128,512]{1,0:T(8,128)}) %reduce-scatter.3.cloned.1.call-update) | async-done | bytes 262160 | tf_op jit(solution)/shard_map/reduce_scatter | solution.py:35
  417.2 1.6 convert_element_type.45
  418.8 79.6 %all-reduce.3.cloned.1.call-done = (bf16[128,512]{1,0:T(8,128)(2,1)}, bf16[128,512]{1,0:T(8,128)(2,1)}) async-done(((bf16[128,512]{1,0:T(8,128)(2,1)}, bf16[128,512]{1,0:T(8,128)(2,1)}), (bf16[128,512]{1,0:T(8,128)(2,1)}, bf16[128,512]{1,0:T(8,128)(2,1)})) %all-reduce.3.cloned.1.call-update) | async-done | bytes 262160 | tf_op jit(solution)/shard_map/psum | solution.py:44
  498.4 4.2 fusion.3
  502.6 3.7 fusion.2
  506.3 0.2 fusion.36
  506.5 1.5 pad_maximum_fusion
  508.0 0.8 pad_maximum_fusion.1
  508.8 0.8 pad_maximum_fusion.2
  (16 shorter events, 0.1 us)
Async XLA Ops:
  13.3 107.8 %copy-start = (bf16[256,4096]{1,0:T(8,128)(2,1)S(1)}, bf16[256,4096]{1,0:T(8,128)(2,1)}, u32[]{:S(2)}) copy-start(bf16[256,4096]{1,0:T(8,128)(2,1)} %param.7) | copy-start | bytes 6291460
  13.3 107.8 %all-to-all-start.1 = ((bf16[32,128,512]{2,1,0:T(8,128)(2,1)}), bf16[32,128,512]{2,1,0:T(8,128)(2,1)}, u32[]{:S(2)}, u32[]{:S(2)}) async-start(bf16[32,128,512]{2,1,0:T(8,128)(2,1)} %stack.30), calls=%async_computation.2 | async-start | bytes 8388608 | tf_op jit(solution)/shard_map/all_to_all | solution.py:30
  25.1 268.6 %reduce-scatter.5.cloned.1.call-start = ((), (), s32[]{:S(2)}) async-start(), calls=%async_computation.5 | async-start | bytes 8650752 | tf_op jit(solution)/shard_map/reduce_scatter | solution.py:35
  132.7 134.3 %all-to-all-start = ((bf16[32,128,512]{2,1,0:T(8,128)(2,1)}), bf16[32,128,512]{2,1,0:T(8,128)(2,1)}, u32[]{:S(2)}, u32[]{:S(2)}) async-start(bf16[32,128,512]{2,1,0:T(8,128)(2,1)} %stack.27), calls=%async_computation | async-start | bytes 8388608 | tf_op jit(solution)/shard_map/all_to_all | solution.py:30
  138.2 278.9 %reduce-scatter.3.cloned.1.call-start = ((), (), s32[]{:S(2)}) async-start(), calls=%async_computation.4 | async-start | bytes 8650752 | tf_op jit(solution)/shard_map/reduce_scatter | solution.py:35
  276.3 222.1 %copy-start.1 = (f32[2,128,512]{2,1,0:T(8,128)S(1)}, f32[2,128,512]{2,1,0:T(8,128)}, u32[]{:S(2)}) copy-start(f32[2,128,512]{2,1,0:T(8,128)} %param.11) | copy-start | bytes 1572868
  276.3 222.1 %copy-start.2 = (f32[2,128,512]{2,1,0:T(8,128)S(1)}, f32[2,128,512]{2,1,0:T(8,128)}, u32[]{:S(2)}) copy-start(f32[2,128,512]{2,1,0:T(8,128)} %param.12) | copy-start | bytes 1572868
  276.3 222.1 %all-reduce.3.cloned.1.call-start = ((), (), s32[]{:S(2)}) async-start(), calls=%async_computation.6 | async-start | bytes 524288 | tf_op jit(solution)/shard_map/psum | solution.py:44
  498.4 4.2 copy-start.3
  498.4 4.2 copy-start.5
  502.6 3.7 copy-start.4
Sparse Core Ops, SparseCore 0:
  130.4 163.2 reduce-scatter.4
  297.7 119.3 reduce-scatter.2
  420.4 77.9 all-reduce.2
